TPU v7x, 32 devices: a whole 2x2x4 slice. The times are simulated.
32 devices in a mesh: grp: 2 (over y), frm: 4 (over z), head: 2 (over x), pos: 2 (over core).
Axes of the slice: x: 2, y: 2, z: 4, core: 2. Of those that a mesh axis runs over, the one named last changes fastest.
Arguments:
- queries: float32 [32, 128, 3072], P(('grp', 'frm'), 'pos', 'head'), parts along dimension 0, may hold values from -120 to 120
- key_states: float32 [32, 128, 3072], P(('grp', 'frm'), 'pos', 'head'), parts along dimension 0, may hold values from -4 to 4
- value_states: float32 [32, 128, 3072], P(('grp', 'frm'), 'pos', 'head'), parts along dimension 0, may hold values from -6 to 6
- windows: int32 [24], P('head'), may hold values from 1 to 2, as said below
- strides: int32 [24], P('head'), may hold values from 4 to 8, as said below
- cutoffs: int32 [24], P('head'), may hold values from 1 to 2, as said below
Outputs:
- blended: float32 [32, 128, 3072], P(('grp', 'frm'), 'pos', 'head'), parts along dimension 0
There are 2 independent parts, one for each index of `grp`. A program takes and returns all parts, laid end to end along the dimension named above; an argument that names none is the same for every part. Nothing has to cross between parts.
Inputs may be any that keep to these rules, and one draw needn't show every extreme that they name: `windows`: some head has exactly 2. `strides`: each is 4 or 8, and both occur. `cutoffs`: some head has exactly 2.
All inputs are finite; a program needn't handle non-finite values.
Results may differ from a plain program's by a relative error of at most 0.0003.
Values sent between devices are 32-bit elements; how exact they have to be, the bound alone decides.
No kernel may reach another device: no remote copies, remote signals or barrier semaphores. Data moves between devices by JAX's collectives and lax.ppermute only.
A program may use at most 128 MiB of HBM per device.

v0:
```python
import math
import jax
import jax.numpy as jnp
from jax import lax
from jax.sharding import PartitionSpec as P

DH = 128
KSTRIDE = 4


def with_halo(value, sides, width):
    for axis, dim in sides:
        size, length = (lax.axis_size(axis), value.shape[dim])
        up = [(i, (i + 1) % size) for i in range(size - 1)]
        down = [(j, i) for i, j in up]
        last = lax.slice_in_dim(value, length - width, length, axis=dim)
        first = lax.slice_in_dim(value, 0, width, axis=dim)
        before = lax.ppermute(last, axis, up)
        after = lax.ppermute(first, axis, down)
        value = jnp.concatenate([before, value, after], axis=dim)
    return value


def attend(query_rows, key_rows, value_rows, allowed, score_scale):
    scores = (
        jnp.einsum("qhd,khd->hqk", query_rows, key_rows, precision=lax.Precision.HIGHEST)
        * score_scale
    )
    highest = jnp.max(jnp.where(allowed, scores, -1e30), axis=2, keepdims=True)
    weights = jnp.where(allowed, jnp.exp(scores - highest), 0.0)
    row_total = jnp.sum(weights, axis=2, keepdims=True)
    return jnp.einsum(
        "hqk,khd->qhd", weights / row_total, value_rows, precision=lax.Precision.HIGHEST
    )


def shards(queries, key_states, value_states, windows, strides, cutoffs):
    frames_dev, half_tokens, channels = queries.shape
    heads_local = channels // DH
    frame_groups = lax.axis_size("frm")
    pos_count = lax.axis_size("pos")
    total_frames = frames_dev * frame_groups
    halo_frames = frames_dev // 2
    score_scale = DH ** (-0.5)
    query_count = frames_dev * half_tokens
    query_rows = queries.reshape(query_count, heads_local, DH)
    query_blocks = queries.reshape(frames_dev, half_tokens, heads_local, DH)
    first_frame = lax.axis_index("frm") * frames_dev
    key_full, value_full = (
        lax.all_gather(key_states, "pos", axis=1, tiled=True),
        lax.all_gather(value_states, "pos", axis=1, tiled=True),
    )
    full_tokens = key_full.shape[1]
    stacked = jnp.stack([key_full, value_full])
    padded = with_halo(stacked, (("frm", 1),), halo_frames)
    window_span = 2 * halo_frames + 1
    span_rows = window_span * full_tokens
    span_offsets = jnp.arange(span_rows, dtype=jnp.int32) // full_tokens - halo_frames

    def local_frame(frame_local):
        query_part = lax.dynamic_index_in_dim(query_blocks, frame_local, 0, keepdims=False)
        block = lax.dynamic_slice_in_dim(padded, frame_local, window_span, 1)
        near_keys = block[0].reshape(span_rows, heads_local, DH)
        near_values = block[1].reshape(span_rows, heads_local, DH)
        near_frames = first_frame + frame_local + span_offsets
        inside = (near_frames >= 0) & (near_frames < total_frames)
        allowed = inside[None, None, :] & (
            jnp.abs(span_offsets)[None, None, :] <= windows[:, None, None]
        )
        return attend(query_part, near_keys, near_values, allowed, score_scale)

    local_out = lax.map(local_frame, jnp.arange(frames_dev, dtype=jnp.int32)).reshape(
        query_count, heads_local, DH
    )
    frame_keys = key_states[::KSTRIDE].reshape(-1, heads_local, DH)
    frame_values = value_states[::KSTRIDE].reshape(-1, heads_local, DH)
    rows_dev = frame_keys.shape[0]
    key_part = lax.all_gather(frame_keys, ("frm", "pos"), axis=0, tiled=True)
    value_part = lax.all_gather(frame_values, ("frm", "pos"), axis=0, tiled=True)
    row_count = key_part.shape[0]
    row_ids = jnp.arange(row_count, dtype=jnp.int32)
    frame_ids = (
        row_ids // rows_dev // pos_count * frames_dev + row_ids % rows_dev // half_tokens * KSTRIDE
    )
    allowed = (frame_ids[None, :] % strides[:, None] == 0)[:, None, :]
    scores = (
        jnp.einsum("qhd,khd->hqk", query_rows, key_part, precision=lax.Precision.HIGHEST)
        * score_scale
    )
    top_old = jnp.full((heads_local, query_count), -1e30, jnp.float32)
    top_new = jnp.maximum(top_old, jnp.max(jnp.where(allowed, scores, -1e30), axis=2))
    weights = jnp.where(allowed, jnp.exp(scores - top_new[:, :, None]), 0.0)
    total_new = jnp.sum(weights, axis=2)
    accum_new = jnp.einsum("hqk,khd->hqd", weights, value_part, precision=lax.Precision.HIGHEST)
    final_state = (top_new, total_new, accum_new)
    top_final, total_final, accum_final = final_state
    global_out = jnp.transpose(accum_final / total_final[:, :, None], (1, 0, 2))
    frequency = jnp.arange(total_frames, dtype=jnp.int32)
    phase_index = frequency[:, None] * frequency[None, :] % total_frames
    phases = 2.0 * math.pi / total_frames * phase_index.astype(jnp.float32)
    cos_table = jnp.cos(phases)
    sin_table = jnp.sin(phases)
    distance_freq = jnp.minimum(frequency, total_frames - frequency)
    low_keep = (distance_freq[None, :] <= cutoffs[:, None]).astype(jnp.float32)
    lowpass = (
        jnp.einsum("kf,hk,kg->hfg", cos_table, low_keep, cos_table, precision=lax.Precision.HIGHEST)
        + jnp.einsum(
            "kf,hk,kg->hfg", sin_table, low_keep, sin_table, precision=lax.Precision.HIGHEST
        )
    ) / total_frames
    group_items = half_tokens // frame_groups
    local_grid = local_out.reshape(frames_dev, frame_groups, group_items, channels)
    global_grid = global_out.reshape(frames_dev, frame_groups, group_items, channels)
    frame_block = lax.all_to_all(
        global_grid - local_grid, "frm", split_axis=1, concat_axis=0, tiled=True
    )
    frames_all = frame_block.shape[0]
    item_count = frame_block.shape[2]
    shaped = frame_block.reshape(frames_all, item_count, heads_local, DH)
    filtered_block = jnp.einsum(
        "hfg,gihd->fihd", lowpass, shaped, precision=lax.Precision.HIGHEST
    ).reshape(frame_block.shape)
    filtered = lax.all_to_all(filtered_block, "frm", split_axis=0, concat_axis=1, tiled=True)
    blended = local_grid + filtered
    return blended.reshape(frames_dev, half_tokens, channels)


def solution(mesh):
    in_specs = (
        P(("grp", "frm"), "pos", "head"),
        P(("grp", "frm"), "pos", "head"),
        P(("grp", "frm"), "pos", "head"),
        P("head"),
        P("head"),
        P("head"),
    )
    out_specs = P(("grp", "frm"), "pos", "head")
    return jax.shard_map(shards, mesh=mesh, in_specs=in_specs, out_specs=out_specs, check_vma=False)
```

profile of v0, /device:TPU:0, one launch (start us, length us, event | category | flops | bytes accessed | tf_op | source)
XLA Modules:
  0.0 456.4 jit_solution(4020904043118848614)
XLA Ops:
  12.1 11.6 %all-gather.5.cloned.1.call-done = f32[4,128,1536]{2,1,0:T(8,128)} async-done(((f32[4,64,1536]{2,1,0:T(8,128)}), f32[4,128,1536]{2,1,0:T(8,128)}) %all-gather.5.cloned.1.call-update) | async-done | bytes 3145744 | tf_op jit(solution)/shard_map/all_gather | solution.py:50
  23.7 14.9 %all-gather.7.cloned.1.call-done = f32[4,128,1536]{2,1,0:T(8,128)} async-done(((f32[4,64,1536]{2,1,0:T(8,128)}), f32[4,128,1536]{2,1,0:T(8,128)}) %all-gather.7.cloned.1.call-update) | async-done | bytes 3145744 | tf_op jit(solution)/shard_map/all_gather | solution.py:51
  38.6 5.9 %fusion.46 = (f32[2,2,128,1536]{3,2,1,0:T(8,128)}, f32[2,2,128,1536]{3,2,1,0:T(8,128)}) fusion(f32[1,4,128,1536]{3,2,1,0:T(8,128)} %bitcast.70, f32[1,4,128,1536]{3,2,1,0:T(8,128)} %bitcast.72), kind=kLoop, calls=%fused_computation.52 | loop fusion | flops 1572864 | bytes 12582912 | tf_op jit(solution)/shard_map/stack | solution.py:54
  56.2 44.0 %all-gather.9.cloned.1.call-done = f32[512,12,128]{2,0,1:T(8,128)} async-done(((f32[64,12,128]{2,0,1:T(8,128)}), f32[512,12,128]{2,0,1:T(8,128)}) %all-gather.9.cloned.1.call-update) | async-done | bytes 3145744 | tf_op jit(solution)/shard_map/all_gather | solution.py:78
  100.3 7.8 %select_reduce_fusion.1 = (f32[12,256]{1,0:T(8,128)S(1)}, f32[12,256,512]{2,1,0:T(8,128)S(1)}) fusion(pred[12,512]{1,0:T(8,128)(4,1)S(1)} %fusion.69, f32[512,12,128]{2,0,1:T(8,128)} %all-gather.9.cloned.1.call-done, f32[256,12,128]{2,1,0:T(8,128)S(1)} %reshape.230), kind=kOutput, calls=%fused_computation.49 | convolution fusion | flops 2420634624 | bytes 11028480 | tf_op jit(solution)/shard_map/qhd,khd->hqk/dot_general | solution.py:87
  112.4 50.4 %all-gather.11.cloned.1.call-done = f32[512,12,128]{2,0,1:T(8,128)} async-done(((f32[64,12,128]{2,0,1:T(8,128)}), f32[512,12,128]{2,0,1:T(8,128)}) %all-gather.11.cloned.1.call-update) | async-done | bytes 3145744 | tf_op jit(solution)/shard_map/all_gather | solution.py:79
  162.8 10.8 %bitcast_divide_fusion = f32[256,12,128]{2,0,1:T(8,128)S(1)} fusion(f32[512,12,128]{2,0,1:T(8,128)} %all-gather.11.cloned.1.call-done, f32[12,256,512]{2,1,0:T(8,128)} %copy-done, f32[12,256]{1,0:T(8,128)S(1)} %broadcast_maximum_fusion, pred[12,512]{1,0:T(8,128)(4,1)S(1)} %fusion.69, f32[256,12]{0,1:T(8,128)S(1)} %bitcast.78), kind=kOutput, calls=%fused_computation.60 | convolution fusion | flops 2421030912 | bytes 11040768 | tf_op jit(solution)/shard_map/hqk,khd->hqd/dot_general | solution.py:94
  178.7 9.5 %pad_maximum_fusion = f32[2,8,128,1536]{3,2,1,0:T(8,128)} fusion(f32[2,2,128,1536]{3,2,1,0:T(8,128)} %collective-permute-done.1, f32[1,4,128,1536]{3,2,1,0:T(8,128)} %bitcast.73, f32[1,4,128,1536]{3,2,1,0:T(8,128)S(1)} %bitcast.71, f32[2,2,128,1536]{3,2,1,0:T(8,128)} %collective-permute-done), kind=kLoop, calls=%fused_computation.45 | loop fusion | flops 9437184 | bytes 25165824 | tf_op jit(solution)/shard_map/concatenate | solution.py:20
  188.3 159.4 %while.12 = (s32[]{:T(128)}, f32[4,64,12,128]{3,1,2,0:T(8,128)}, s32[4]{0:T(128)S(1)}, f32[2,8,128,1536]{3,2,1,0:T(8,128)}, s32[]{:T(128)}, /*index=5*/s32[12]{0...) while((s32[]{:T(128)}, f32[4,64,12,128]{3,1,2,0:T(8,128)}, ...), condition=%wide.region_3.4_spmd.clone, body=%wide.region_0.3_spmd.clone.sunk | while | flops 1513420800 | bytes 58486832 | solution.py:72
  190.4 7.1 %constant_dynamic-slice_fusion.3 = (f32[1,5,128,1536]{3,2,1,0:T(8,128)}, f32[1,5,128,1536]{3,2,1,0:T(8,128)}) fusion(f32[2,8,128,1536]{3,2,1,0:T(8,128)} %get-tuple-element.216, s32[]{:T(128)S(6)} %add.172, s32[]{:T(128)S(6)} %select_n.212), kind=kLoop, calls=%fused_computation.41.clone.1 | loop fusion | bytes 15728648 | tf_op jit(solution)/shard_map/while/body/eval_jaxpr/slice | solution.py:64
  204.0 8.7 %fusion.129 = f32[12,64,640]{2,1,0:T(8,128)S(1)} fusion(f32[640,12,128]{2,1,0:T(8,128)} %squeeze.24, f32[4,64,12,128]{3,1,2,0:T(8,128)} %get-tuple-element.219, s32[]{:T(128)S(6)} %select_n.213), kind=kOutput, calls=%fused_computation.5.clone.1 | convolution fusion | flops 754974720 | bytes 7602180 | tf_op jit(solution)/shard_map/while/body/eval_jaxpr/qhd,khd->hqk/dot_general | solution.py:26
  220.8 7.3 %fusion.133 = f32[4,64,12,128]{3,1,2,0:T(8,128)} fusion(f32[4,64,12,128]{3,1,2,0:T(8,128)} %get-tuple-element.202, s32[]{:T(128)} %get-tuple-element.201, f32[12,64,640]{2,1,0:T(8,128)S(1)} %copy-done.7, f32[640,12,128]{2,1,0:T(8,128)} %squeeze.25, f32[12,64]{1,0:T(8,128)S(1)} %get-tuple-element.188), kind=kOutput, calls=%fused_computation.13.clone.1 | convolution fusion | flops 755466240 | bytes 7605760 | tf_op jit(solution)/shard_map/while/body/eval_jaxpr/hqk,khd->qhd/dot_general | solution.py:32
  230.3 7.1 %constant_dynamic-slice_fusion.3 = (f32[1,5,128,1536]{3,2,1,0:T(8,128)}, f32[1,5,128,1536]{3,2,1,0:T(8,128)}) fusion(f32[2,8,128,1536]{3,2,1,0:T(8,128)} %get-tuple-element.216, s32[]{:T(128)S(6)} %add.172, s32[]{:T(128)S(6)} %select_n.212), kind=kLoop, calls=%fused_computation.41.clone.1 | loop fusion | bytes 15728648 | tf_op jit(solution)/shard_map/while/body/eval_jaxpr/slice | solution.py:64
  243.9 8.7 %fusion.129 = f32[12,64,640]{2,1,0:T(8,128)S(1)} fusion(f32[640,12,128]{2,1,0:T(8,128)} %squeeze.24, f32[4,64,12,128]{3,1,2,0:T(8,128)} %get-tuple-element.219, s32[]{:T(128)S(6)} %select_n.213), kind=kOutput, calls=%fused_computation.5.clone.1 | convolution fusion | flops 754974720 | bytes 7602180 | tf_op jit(solution)/shard_map/while/body/eval_jaxpr/qhd,khd->hqk/dot_general | solution.py:26
  260.7 7.2 %fusion.133 = f32[4,64,12,128]{3,1,2,0:T(8,128)} fusion(f32[4,64,12,128]{3,1,2,0:T(8,128)} %get-tuple-element.202, s32[]{:T(128)} %get-tuple-element.201, f32[12,64,640]{2,1,0:T(8,128)S(1)} %copy-done.7, f32[640,12,128]{2,1,0:T(8,128)} %squeeze.25, f32[12,64]{1,0:T(8,128)S(1)} %get-tuple-element.188), kind=kOutput, calls=%fused_computation.13.clone.1 | convolution fusion | flops 755466240 | bytes 7605760 | tf_op jit(solution)/shard_map/while/body/eval_jaxpr/hqk,khd->qhd/dot_general | solution.py:32
  270.1 7.1 %constant_dynamic-slice_fusion.3 = (f32[1,5,128,1536]{3,2,1,0:T(8,128)}, f32[1,5,128,1536]{3,2,1,0:T(8,128)}) fusion(f32[2,8,128,1536]{3,2,1,0:T(8,128)} %get-tuple-element.216, s32[]{:T(128)S(6)} %add.172, s32[]{:T(128)S(6)} %select_n.212), kind=kLoop, calls=%fused_computation.41.clone.1 | loop fusion | bytes 15728648 | tf_op jit(solution)/shard_map/while/body/eval_jaxpr/slice | solution.py:64
  283.7 8.7 %fusion.129 = f32[12,64,640]{2,1,0:T(8,128)S(1)} fusion(f32[640,12,128]{2,1,0:T(8,128)} %squeeze.24, f32[4,64,12,128]{3,1,2,0:T(8,128)} %get-tuple-element.219, s32[]{:T(128)S(6)} %select_n.213), kind=kOutput, calls=%fused_computation.5.clone.1 | convolution fusion | flops 754974720 | bytes 7602180 | tf_op jit(solution)/shard_map/while/body/eval_jaxpr/qhd,khd->hqk/dot_general | solution.py:26
  300.5 7.2 %fusion.133 = f32[4,64,12,128]{3,1,2,0:T(8,128)} fusion(f32[4,64,12,128]{3,1,2,0:T(8,128)} %get-tuple-element.202, s32[]{:T(128)} %get-tuple-element.201, f32[12,64,640]{2,1,0:T(8,128)S(1)} %copy-done.7, f32[640,12,128]{2,1,0:T(8,128)} %squeeze.25, f32[12,64]{1,0:T(8,128)S(1)} %get-tuple-element.188), kind=kOutput, calls=%fused_computation.13.clone.1 | convolution fusion | flops 755466240 | bytes 7605760 | tf_op jit(solution)/shard_map/while/body/eval_jaxpr/hqk,khd->qhd/dot_general | solution.py:32
  310.0 7.1 %constant_dynamic-slice_fusion.3 = (f32[1,5,128,1536]{3,2,1,0:T(8,128)}, f32[1,5,128,1536]{3,2,1,0:T(8,128)}) fusion(f32[2,8,128,1536]{3,2,1,0:T(8,128)} %get-tuple-element.216, s32[]{:T(128)S(6)} %add.172, s32[]{:T(128)S(6)} %select_n.212), kind=kLoop, calls=%fused_computation.41.clone.1 | loop fusion | bytes 15728648 | tf_op jit(solution)/shard_map/while/body/eval_jaxpr/slice | solution.py:64
  323.5 8.7 %fusion.129 = f32[12,64,640]{2,1,0:T(8,128)S(1)} fusion(f32[640,12,128]{2,1,0:T(8,128)} %squeeze.24, f32[4,64,12,128]{3,1,2,0:T(8,128)} %get-tuple-element.219, s32[]{:T(128)S(6)} %select_n.213), kind=kOutput, calls=%fused_computation.5.clone.1 | convolution fusion | flops 754974720 | bytes 7602180 | tf_op jit(solution)/shard_map/while/body/eval_jaxpr/qhd,khd->hqk/dot_general | solution.py:26
  340.4 7.2 %fusion.133 = f32[4,64,12,128]{3,1,2,0:T(8,128)} fusion(f32[4,64,12,128]{3,1,2,0:T(8,128)} %get-tuple-element.202, s32[]{:T(128)} %get-tuple-element.201, f32[12,64,640]{2,1,0:T(8,128)S(1)} %copy-done.7, f32[640,12,128]{2,1,0:T(8,128)} %squeeze.25, f32[12,64]{1,0:T(8,128)S(1)} %get-tuple-element.188), kind=kOutput, calls=%fused_computation.13.clone.1 | convolution fusion | flops 755466240 | bytes 7605760 | tf_op jit(solution)/shard_map/while/body/eval_jaxpr/hqk,khd->qhd/dot_general | solution.py:32
  354.8 7.4 %all-to-all-start = ((f32[4,4,16,1536]{3,2,0,1:T(8,128)}), f32[4,4,16,1536]{3,2,0,1:T(8,128)S(1)}, u32[]{:S(2)}, u32[]{:S(2)}) async-start(f32[4,4,16,1536]{3,2,0,1:T(8,128)} %copy.33), calls=%async_computation | async-start | bytes 3145728 | tf_op jit(solution)/shard_map/all_to_all | solution.py:114
  363.1 36.4 %all-to-all-done = f32[4,4,16,1536]{3,2,0,1:T(8,128)S(1)} async-done(((f32[4,4,16,1536]{3,2,0,1:T(8,128)}), f32[4,4,16,1536]{3,2,0,1:T(8,128)S(1)}, u32[]{:S(2)}, u32[]{:S(2)}) %all-to-all-start) | async-done | bytes 1572896 | tf_op jit(solution)/shard_map/all_to_all | solution.py:114
  407.0 40.1 %all_to_all.33 = f32[16,1,16,1536]{3,2,1,0:T(8,128)S(1)} all-to-all(f32[16,1,16,1536]{3,2,1,0:T(8,128)} %bitcast.75), channel_id=1, replica_groups=mesh['grp'=2,'frm'=4,'head'=2,'pos'=2] {'frm'}, dimensions={0} | all-to-all | bytes 3145728 | tf_op jit(solution)/shard_map/all_to_all | solution.py:123
  (98 shorter events, 98.7 us)
Async XLA Ops:
  6.5 17.2 %all-gather.5.cloned.1.call-start = ((), (), s32[]{:S(2)}) async-start(), calls=%async_computation.2 | async-start | bytes 4718592 | tf_op jit(solution)/shard_map/all_gather | solution.py:50
  7.3 31.4 %all-gather.7.cloned.1.call-start = ((), (), s32[]{:S(2)}) async-start(), calls=%async_computation.3 | async-start | bytes 4718592 | tf_op jit(solution)/shard_map/all_gather | solution.py:51
  8.0 92.3 %all-gather.9.cloned.1.call-start = ((), (), s32[]{:S(2)}) async-start(), calls=%async_computation.4 | async-start | bytes 3538944 | tf_op jit(solution)/shard_map/all_gather | solution.py:78
  10.1 152.7 %all-gather.11.cloned.1.call-start = ((), (), s32[]{:S(2)}) async-start(), calls=%async_computation.5 | async-start | bytes 3538944 | tf_op jit(solution)/shard_map/all_gather | solution.py:79
  44.6 8.3 %copy-start.6 = (s32[12]{0:T(128)S(1)}, s32[12]{0:T(128)}, u32[]{:S(2)}) copy-start(s32[12]{0:T(128)} %param.12) | copy-start | bytes 148
  44.6 134.1 %collective-permute-start = (f32[2,2,128,1536]{3,2,1,0:T(8,128)}, f32[2,2,128,1536]{3,2,1,0:T(8,128)}, u32[]{:S(2)}, u32[]{:S(2)}) collective-permute-start(f32[2,2,128,1536]{3,2,1,0:T(8,128)} %get-tuple-element.134), channel_id=1, source_target_pairs={{0,4},{4,8},{8,12},{1,5},{5,9},{9,13},{2,6},{6,10},{10,14},{3,7},{... | collective-permute-start | bytes 9437192 | tf_op jit(solution)/shard_map/ppermute | solution.py:18
  50.0 128.6 %collective-permute-start.1 = (f32[2,2,128,1536]{3,2,1,0:T(8,128)}, f32[2,2,128,1536]{3,2,1,0:T(8,128)}, u32[]{:S(2)}, u32[]{:S(2)}) collective-permute-start(f32[2,2,128,1536]{3,2,1,0:T(8,128)} %get-tuple-element.135), channel_id=1, source_target_pairs={{4,0},{8,4},{12,8},{5,1},{9,5},{13,9},{6,2},{10,6},{14,10},{7,3},{... | collective-permute-start | bytes 9437192 | tf_op jit(solution)/shard_map/ppermute | solution.py:19
  108.1 2.6 copy-start
  175.9 2.7 copy-start.1
  178.7 9.6 %copy-start.4 = (s32[12]{0:T(128)S(1)}, s32[12]{0:T(128)}, u32[]{:S(2)}) copy-start(s32[12]{0:T(128)} %param.11) | copy-start | bytes 148
  215.3 5.5 %copy-start.7 = (f32[12,64,640]{2,1,0:T(8,128)S(1)}, f32[12,64,640]{2,1,0:T(8,128)}, u32[]{:S(2)}) copy-start(f32[12,64,640]{2,1,0:T(8,128)} %get-tuple-element.186) | copy-start | bytes 5898244 | tf_op jit(solution)/shard_map/while
  255.2 5.5 %copy-start.7 = (f32[12,64,640]{2,1,0:T(8,128)S(1)}, f32[12,64,640]{2,1,0:T(8,128)}, u32[]{:S(2)}) copy-start(f32[12,64,640]{2,1,0:T(8,128)} %get-tuple-element.186) | copy-start | bytes 5898244 | tf_op jit(solution)/shard_map/while
  295.0 5.5 %copy-start.7 = (f32[12,64,640]{2,1,0:T(8,128)S(1)}, f32[12,64,640]{2,1,0:T(8,128)}, u32[]{:S(2)}) copy-start(f32[12,64,640]{2,1,0:T(8,128)} %get-tuple-element.186) | copy-start | bytes 5898244 | tf_op jit(solution)/shard_map/while
  334.9 5.5 %copy-start.7 = (f32[12,64,640]{2,1,0:T(8,128)S(1)}, f32[12,64,640]{2,1,0:T(8,128)}, u32[]{:S(2)}) copy-start(f32[12,64,640]{2,1,0:T(8,128)} %get-tuple-element.186) | copy-start | bytes 5898244 | tf_op jit(solution)/shard_map/while
  354.8 7.7 %copy-start.5 = (s32[12]{0:T(128)S(1)}, s32[12]{0:T(128)}, u32[]{:S(2)}) copy-start(s32[12]{0:T(128)} %param.13) | copy-start | bytes 148
  354.8 44.8 %all-to-all-start = ((f32[4,4,16,1536]{3,2,0,1:T(8,128)}), f32[4,4,16,1536]{3,2,0,1:T(8,128)S(1)}, u32[]{:S(2)}, u32[]{:S(2)}) async-start(f32[4,4,16,1536]{3,2,0,1:T(8,128)} %copy.33), calls=%async_computation | async-start | bytes 3145728 | tf_op jit(solution)/shard_map/all_to_all | solution.py:114
  399.5 1.1 copy-start.3
  447.1 1.4 copy-start.2
Sparse Core Ops, SparseCore 0:
  8.9 14.8 all-gather.4
  25.3 13.2 all-gather.6
  40.2 59.9 all-gather.8
  101.7 61.0 all-gather.10
where the time goes:
time: 458 us; the launch traced here: 456 us
  waiting for transfers between devices  159 us (35%)
  local copies, waits for them, and re-layouts  102 us (22%)
  matrix products  85.3 us (19%)
  blocking collectives  40.1 us (9%)
  other arithmetic  29.7 us (6%)
  starting transfers between devices  14.3 us (3%)
  loops' own time  13.3 us (3%)
  between operations  13.3 us (3%)
    all_gather x1, waiting for transfers between devices, shards(): lax.all_gather(frame_values, ('frm', 'pos'), axis=0, tiled=True)  50.4 us
    all_gather x1, waiting for transfers between devices, shards(): key_part = lax.all_gather(frame_keys, ('frm', 'pos'), axis=0, tiled=True)  44 us
    all_to_all x1, blocking collectives, shards(): lax.all_to_all(filtered_block, 'frm', split_axis=0, concat_axis=1, tiled=...  40.1 us
    all_to_all x1, waiting for transfers between devices, shards(): lax.all_to_all(global_grid - local_grid, 'frm', split_axis=1, concat_axis...  36.4 us
    dot_general x4, matrix products, attend(): jnp.einsum('qhd,khd->hqk', query_rows, key_rows, precision=lax.Precision....  34.7 us
    dot_general x4, matrix products, attend(): jnp.einsum('hqk,khd->qhd', weights / row_total, value_rows, precision=lax...  29 us
    slice x4, local copies, waits for them, and re-layouts, local_frame(): near_values = block[1].reshape(span_rows, heads_local, DH)  28.4 us
    squeeze x4, local copies, waits for them, and re-layouts, local_frame(): near_values = block[1].reshape(span_rows, heads_local, DH)  22 us
  transfers between devices with their start and end apart: 7, of which 5 were waited for; matrix products, arithmetic and copies ran while one was open for 9% of the time, Pallas kernels for 0%

commit v1 on v0

--- a/solution.py
+++ b/solution.py
@@ -75,8 +75,13 @@
     frame_keys = key_states[::KSTRIDE].reshape(-1, heads_local, DH)
     frame_values = value_states[::KSTRIDE].reshape(-1, heads_local, DH)
     rows_dev = frame_keys.shape[0]
-    key_part = lax.all_gather(frame_keys, ("frm", "pos"), axis=0, tiled=True)
-    value_part = lax.all_gather(frame_values, ("frm", "pos"), axis=0, tiled=True)
+    key_part, value_part = jnp.split(
+        lax.all_gather(
+            jnp.concatenate([frame_keys, frame_values], axis=1), ("frm", "pos"), axis=0, tiled=True
+        ),
+        [frame_keys.shape[1]],
+        axis=1,
+    )
     row_count = key_part.shape[0]
     row_ids = jnp.arange(row_count, dtype=jnp.int32)
     frame_ids = (

time: 458 us -> 477 us (1.041)
  waiting for transfers between devices: 159 us -> 180 us
  local copies, waits for them, and re-layouts: 102 us -> 97 us
    ppermute x1, waiting for transfers between devices: 0.01 us -> 107 us  [with_halo(): before = lax.ppermute(last, axis, up)]
    all_gather x2 -> x1, waiting for transfers between devices: 94.5 us -> 0.01 us  [shards(): lax.all_gather(jnp.concatenate([frame_keys, frame_values], axis=1), ('frm...]
    ppermute x1, waiting for transfers between devices: 0.01 us -> 5.81 us  [with_halo(): after = lax.ppermute(first, axis, down)]
  transfers between devices with their start and end apart: 7 -> 6, of which waited for: 5 -> 5; matrix products, arithmetic and copies ran while one was open for 9% -> 36% of each run, Pallas kernels for 0% -> 0%
where the time goes in v1:
time: 477 us; the launch traced here: 475 us
  waiting for transfers between devices  180 us (38%)
  local copies, waits for them, and re-layouts  97 us (20%)
  matrix products  87.5 us (18%)
  blocking collectives  40 us (8%)
  other arithmetic  30.7 us (6%)
  between operations  15.1 us (3%)
  loops' own time  14.7 us (3%)
  starting transfers between devices  10.7 us (2%)
    ppermute x1, waiting for transfers between devices, with_halo(): before = lax.ppermute(last, axis, up)  107 us
    all_to_all x1, blocking collectives, shards(): lax.all_to_all(filtered_block, 'frm', split_axis=0, concat_axis=1, tiled=...  40 us
    all_to_all x1, waiting for transfers between devices, shards(): lax.all_to_all(global_grid - local_grid, 'frm', split_axis=1, concat_axis...  35.3 us
    dot_general x4, matrix products, attend(): jnp.einsum('qhd,khd->hqk', query_rows, key_rows, precision=lax.Precision....  34.7 us
    dot_general x4, matrix products, attend(): jnp.einsum('hqk,khd->qhd', weights / row_total, value_rows, precision=lax...  29 us
    slice x4, local copies, waits for them, and re-layouts, local_frame(): near_values = block[1].reshape(span_rows, heads_local, DH)  28.5 us
    squeeze x4, local copies, waits for them, and re-layouts, local_frame(): near_values = block[1].reshape(span_rows, heads_local, DH)  22 us
    squeeze x4, local copies, waits for them, and re-layouts, local_frame(): near_keys = block[0].reshape(span_rows, heads_local, DH)  21.4 us
  transfers between devices with their start and end apart: 6, of which 5 were waited for; matrix products, arithmetic and copies ran while one was open for 36% of the time, Pallas kernels for 0%

profile of v1, /device:TPU:0, one launch (start us, length us, event | category | flops | bytes accessed | tf_op | source)
XLA Modules:
  0.0 475.5 jit_solution(10366215553692008814)
XLA Ops:
  8.9 15.7 %all-gather.4.cloned.1.call-done = f32[4,128,1536]{2,1,0:T(8,128)} async-done(((f32[4,64,1536]{2,1,0:T(8,128)}), f32[4,128,1536]{2,1,0:T(8,128)}) %all-gather.4.cloned.1.call-update) | async-done | bytes 3145744 | tf_op jit(solution)/shard_map/all_gather | solution.py:50
  24.6 14.9 %all-gather.6.cloned.1.call-done = f32[4,128,1536]{2,1,0:T(8,128)} async-done(((f32[4,64,1536]{2,1,0:T(8,128)}), f32[4,128,1536]{2,1,0:T(8,128)}) %all-gather.6.cloned.1.call-update) | async-done | bytes 3145744 | tf_op jit(solution)/shard_map/all_gather | solution.py:51
  39.4 6.0 %fusion.46 = (f32[2,2,128,1536]{3,2,1,0:T(8,128)}, f32[2,2,128,1536]{3,2,1,0:T(8,128)}) fusion(f32[1,4,128,1536]{3,2,1,0:T(8,128)} %bitcast.69, f32[1,4,128,1536]{3,2,1,0:T(8,128)} %bitcast.71), kind=kLoop, calls=%fused_computation.52 | loop fusion | flops 1572864 | bytes 12582912 | tf_op jit(solution)/shard_map/stack | solution.py:54
  61.1 106.6 %collective-permute-done = f32[2,2,128,1536]{3,2,1,0:T(8,128)} collective-permute-done((f32[2,2,128,1536]{3,2,1,0:T(8,128)}, f32[2,2,128,1536]{3,2,1,0:T(8,128)}, u32[]{:S(2)}, u32[]{:S(2)}) %collective-permute-start) | collective-permute-done | bytes 3145760 | tf_op jit(solution)/shard_map/ppermute | solution.py:18
  167.7 5.8 %collective-permute-done.1 = f32[2,2,128,1536]{3,2,1,0:T(8,128)} collective-permute-done((f32[2,2,128,1536]{3,2,1,0:T(8,128)}, f32[2,2,128,1536]{3,2,1,0:T(8,128)}, u32[]{:S(2)}, u32[]{:S(2)}) %collective-permute-start.1) | collective-permute-done | bytes 3145760 | tf_op jit(solution)/shard_map/ppermute | solution.py:19
  173.6 9.6 %pad_maximum_fusion = f32[2,8,128,1536]{3,2,1,0:T(8,128)} fusion(f32[2,2,128,1536]{3,2,1,0:T(8,128)} %collective-permute-done.1, f32[1,4,128,1536]{3,2,1,0:T(8,128)} %bitcast.72, f32[1,4,128,1536]{3,2,1,0:T(8,128)S(1)} %bitcast.70, f32[2,2,128,1536]{3,2,1,0:T(8,128)} %collective-permute-done), kind=kLoop, calls=%fused_computation.45 | loop fusion | flops 9437184 | bytes 25165824 | tf_op jit(solution)/shard_map/concatenate | solution.py:20
  183.2 161.4 %while.12 = (s32[]{:T(128)}, f32[4,64,12,128]{3,1,2,0:T(8,128)}, s32[4]{0:T(128)S(1)}, f32[2,8,128,1536]{3,2,1,0:T(8,128)}, s32[]{:T(128)}, /*index=5*/s32[12]{0...) while((s32[]{:T(128)}, f32[4,64,12,128]{3,1,2,0:T(8,128)}, ...), condition=%wide.region_3.4_spmd.clone, body=%wide.region_0.3_spmd.clone.sunk | while | flops 1513420800 | bytes 58486832 | solution.py:72
  185.6 7.1 %constant_dynamic-slice_fusion.3 = (f32[1,5,128,1536]{3,2,1,0:T(8,128)}, f32[1,5,128,1536]{3,2,1,0:T(8,128)}) fusion(f32[2,8,128,1536]{3,2,1,0:T(8,128)} %get-tuple-element.216, s32[]{:T(128)S(6)} %add.172, s32[]{:T(128)S(6)} %select_n.214), kind=kLoop, calls=%fused_computation.41.clone.1 | loop fusion | bytes 15728648 | tf_op jit(solution)/shard_map/while/body/eval_jaxpr/slice | solution.py:64
  199.3 8.7 %fusion.131 = f32[12,64,640]{2,1,0:T(8,128)S(1)} fusion(f32[640,12,128]{2,1,0:T(8,128)} %squeeze.24, f32[4,64,12,128]{3,1,2,0:T(8,128)} %get-tuple-element.219, s32[]{:T(128)S(6)} %select_n.215), kind=kOutput, calls=%fused_computation.5.clone.1 | convolution fusion | flops 754974720 | bytes 7602180 | tf_op jit(solution)/shard_map/while/body/eval_jaxpr/qhd,khd->hqk/dot_general | solution.py:26
  216.2 7.3 %fusion.135 = f32[4,64,12,128]{3,1,2,0:T(8,128)} fusion(f32[4,64,12,128]{3,1,2,0:T(8,128)} %get-tuple-element.202, s32[]{:T(128)} %get-tuple-element.201, f32[12,64,640]{2,1,0:T(8,128)S(1)} %copy-done.8, f32[640,12,128]{2,1,0:T(8,128)} %squeeze.25, f32[12,64]{1,0:T(8,128)S(1)} %get-tuple-element.188), kind=kOutput, calls=%fused_computation.13.clone.1 | convolution fusion | flops 755466240 | bytes 7605760 | tf_op jit(solution)/shard_map/while/body/eval_jaxpr/hqk,khd->qhd/dot_general | solution.py:32
  225.9 7.1 %constant_dynamic-slice_fusion.3 = (f32[1,5,128,1536]{3,2,1,0:T(8,128)}, f32[1,5,128,1536]{3,2,1,0:T(8,128)}) fusion(f32[2,8,128,1536]{3,2,1,0:T(8,128)} %get-tuple-element.216, s32[]{:T(128)S(6)} %add.172, s32[]{:T(128)S(6)} %select_n.214), kind=kLoop, calls=%fused_computation.41.clone.1 | loop fusion | bytes 15728648 | tf_op jit(solution)/shard_map/while/body/eval_jaxpr/slice | solution.py:64
  239.6 8.7 %fusion.131 = f32[12,64,640]{2,1,0:T(8,128)S(1)} fusion(f32[640,12,128]{2,1,0:T(8,128)} %squeeze.24, f32[4,64,12,128]{3,1,2,0:T(8,128)} %get-tuple-element.219, s32[]{:T(128)S(6)} %select_n.215), kind=kOutput, calls=%fused_computation.5.clone.1 | convolution fusion | flops 754974720 | bytes 7602180 | tf_op jit(solution)/shard_map/while/body/eval_jaxpr/qhd,khd->hqk/dot_general | solution.py:26
  256.6 7.3 %fusion.135 = f32[4,64,12,128]{3,1,2,0:T(8,128)} fusion(f32[4,64,12,128]{3,1,2,0:T(8,128)} %get-tuple-element.202, s32[]{:T(128)} %get-tuple-element.201, f32[12,64,640]{2,1,0:T(8,128)S(1)} %copy-done.8, f32[640,12,128]{2,1,0:T(8,128)} %squeeze.25, f32[12,64]{1,0:T(8,128)S(1)} %get-tuple-element.188), kind=kOutput, calls=%fused_computation.13.clone.1 | convolution fusion | flops 755466240 | bytes 7605760 | tf_op jit(solution)/shard_map/while/body/eval_jaxpr/hqk,khd->qhd/dot_general | solution.py:32
  266.3 7.1 %constant_dynamic-slice_fusion.3 = (f32[1,5,128,1536]{3,2,1,0:T(8,128)}, f32[1,5,128,1536]{3,2,1,0:T(8,128)}) fusion(f32[2,8,128,1536]{3,2,1,0:T(8,128)} %get-tuple-element.216, s32[]{:T(128)S(6)} %add.172, s32[]{:T(128)S(6)} %select_n.214), kind=kLoop, calls=%fused_computation.41.clone.1 | loop fusion | bytes 15728648 | tf_op jit(solution)/shard_map/while/body/eval_jaxpr/slice | solution.py:64
  280.0 8.7 %fusion.131 = f32[12,64,640]{2,1,0:T(8,128)S(1)} fusion(f32[640,12,128]{2,1,0:T(8,128)} %squeeze.24, f32[4,64,12,128]{3,1,2,0:T(8,128)} %get-tuple-element.219, s32[]{:T(128)S(6)} %select_n.215), kind=kOutput, calls=%fused_computation.5.clone.1 | convolution fusion | flops 754974720 | bytes 7602180 | tf_op jit(solution)/shard_map/while/body/eval_jaxpr/qhd,khd->hqk/dot_general | solution.py:26
  291.4 5.5 %squeeze.25 = f32[640,12,128]{2,1,0:T(8,128)} reshape(f32[1,5,128,1536]{3,2,1,0:T(8,128)} %get-tuple-element.187) | data formatting | bytes 7864320 | tf_op jit(solution)/shard_map/while/body/eval_jaxpr/reshape;while/body/eval_jaxpr/squeeze | solution.py:64
  296.9 7.3 %fusion.135 = f32[4,64,12,128]{3,1,2,0:T(8,128)} fusion(f32[4,64,12,128]{3,1,2,0:T(8,128)} %get-tuple-element.202, s32[]{:T(128)} %get-tuple-element.201, f32[12,64,640]{2,1,0:T(8,128)S(1)} %copy-done.8, f32[640,12,128]{2,1,0:T(8,128)} %squeeze.25, f32[12,64]{1,0:T(8,128)S(1)} %get-tuple-element.188), kind=kOutput, calls=%fused_computation.13.clone.1 | convolution fusion | flops 755466240 | bytes 7605760 | tf_op jit(solution)/shard_map/while/body/eval_jaxpr/hqk,khd->qhd/dot_general | solution.py:32
  306.6 7.1 %constant_dynamic-slice_fusion.3 = (f32[1,5,128,1536]{3,2,1,0:T(8,128)}, f32[1,5,128,1536]{3,2,1,0:T(8,128)}) fusion(f32[2,8,128,1536]{3,2,1,0:T(8,128)} %get-tuple-element.216, s32[]{:T(128)S(6)} %add.172, s32[]{:T(128)S(6)} %select_n.214), kind=kLoop, calls=%fused_computation.41.clone.1 | loop fusion | bytes 15728648 | tf_op jit(solution)/shard_map/while/body/eval_jaxpr/slice | solution.py:64
  320.3 8.7 %fusion.131 = f32[12,64,640]{2,1,0:T(8,128)S(1)} fusion(f32[640,12,128]{2,1,0:T(8,128)} %squeeze.24, f32[4,64,12,128]{3,1,2,0:T(8,128)} %get-tuple-element.219, s32[]{:T(128)S(6)} %select_n.215), kind=kOutput, calls=%fused_computation.5.clone.1 | convolution fusion | flops 754974720 | bytes 7602180 | tf_op jit(solution)/shard_map/while/body/eval_jaxpr/qhd,khd->hqk/dot_general | solution.py:26
  337.3 7.2 %fusion.135 = f32[4,64,12,128]{3,1,2,0:T(8,128)} fusion(f32[4,64,12,128]{3,1,2,0:T(8,128)} %get-tuple-element.202, s32[]{:T(128)} %get-tuple-element.201, f32[12,64,640]{2,1,0:T(8,128)S(1)} %copy-done.8, f32[640,12,128]{2,1,0:T(8,128)} %squeeze.25, f32[12,64]{1,0:T(8,128)S(1)} %get-tuple-element.188), kind=kOutput, calls=%fused_computation.13.clone.1 | convolution fusion | flops 755466240 | bytes 7605760 | tf_op jit(solution)/shard_map/while/body/eval_jaxpr/hqk,khd->qhd/dot_general | solution.py:32
  348.3 8.7 %select_reduce_fusion.1 = (f32[12,256]{1,0:T(8,128)S(1)}, f32[12,512,256]{2,1,0:T(8,128)S(1)}) fusion(pred[12,512]{1,0:T(8,128)(4,1)S(1)} %fusion.72, f32[512,24,128]{2,0,1:T(8,128)} %all-gather.8.cloned.1.call-done, f32[256,12,128]{2,1,0:T(8,128)} %reshape.232), kind=kOutput, calls=%fused_computation.49 | convolution fusion | flops 2420634624 | bytes 14174208 | tf_op jit(solution)/shard_map/qhd,khd->hqk/dot_general | solution.py:92
  359.8 12.1 %bitcast_divide_fusion = f32[256,12,128]{2,0,1:T(8,128)S(1)} fusion(f32[512,24,128]{2,0,1:T(8,128)S(1)} %copy-done, f32[12,512,256]{2,1,0:T(8,128)S(1)} %get-tuple-element.137, f32[12,256]{1,0:T(8,128)S(1)} %broadcast_maximum_fusion, pred[12,512]{1,0:T(8,128)(4,1)S(1)} %fusion.72, f32[256,12]{0,1:T(8,128)S(1)} %bitcast.77), kind=kOutput, calls=%fused_computation.61 | convolution fusion | flops 2421030912 | bytes 11051008 | tf_op jit(solution)/shard_map/hqk,khd->hqd/dot_general | solution.py:99
  382.4 35.3 %all-to-all-done = f32[4,4,16,1536]{3,2,0,1:T(8,128)S(1)} async-done(((f32[4,4,16,1536]{3,2,0,1:T(8,128)}), f32[4,4,16,1536]{3,2,0,1:T(8,128)S(1)}, u32[]{:S(2)}, u32[]{:S(2)}) %all-to-all-start) | async-done | bytes 1572896 | tf_op jit(solution)/shard_map/all_to_all | solution.py:119
  425.3 40.0 %all_to_all.33 = f32[16,1,16,1536]{3,2,1,0:T(8,128)S(1)} all-to-all(f32[16,1,16,1536]{3,2,1,0:T(8,128)} %bitcast.74), channel_id=1, replica_groups=mesh['grp'=2,'frm'=4,'head'=2,'pos'=2] {'frm'}, dimensions={0} | all-to-all | bytes 3145728 | tf_op jit(solution)/shard_map/all_to_all | solution.py:128
  (98 shorter events, 93.3 us)
Async XLA Ops:
  7.4 17.2 %all-gather.4.cloned.1.call-start = ((), (), s32[]{:S(2)}) async-start(), calls=%async_computation.2 | async-start | bytes 4718592 | tf_op jit(solution)/shard_map/all_gather | solution.py:50
  8.1 31.4 %all-gather.6.cloned.1.call-start = ((), (), s32[]{:S(2)}) async-start(), calls=%async_computation.3 | async-start | bytes 4718592 | tf_op jit(solution)/shard_map/all_gather | solution.py:51
  8.8 339.4 %all-gather.8.cloned.1.call-start = ((), (), s32[]{:S(2)}) async-start(), calls=%async_computation.4 | async-start | bytes 7077888 | tf_op jit(solution)/shard_map/all_gather | solution.py:79
  45.4 122.3 %collective-permute-start = (f32[2,2,128,1536]{3,2,1,0:T(8,128)}, f32[2,2,128,1536]{3,2,1,0:T(8,128)}, u32[]{:S(2)}, u32[]{:S(2)}) collective-permute-start(f32[2,2,128,1536]{3,2,1,0:T(8,128)} %get-tuple-element.134), channel_id=1, source_target_pairs={{0,4},{4,8},{8,12},{1,5},{5,9},{9,13},{2,6},{6,10},{10,14},{3,7},{... | collective-permute-start | bytes 9437192 | tf_op jit(solution)/shard_map/ppermute | solution.py:18
  50.8 122.8 %collective-permute-start.1 = (f32[2,2,128,1536]{3,2,1,0:T(8,128)}, f32[2,2,128,1536]{3,2,1,0:T(8,128)}, u32[]{:S(2)}, u32[]{:S(2)}) collective-permute-start(f32[2,2,128,1536]{3,2,1,0:T(8,128)} %get-tuple-element.135), channel_id=1, source_target_pairs={{4,0},{8,4},{12,8},{5,1},{9,5},{13,9},{6,2},{10,6},{14,10},{7,3},{... | collective-permute-start | bytes 9437192 | tf_op jit(solution)/shard_map/ppermute | solution.py:19
  54.3 1.7 copy-start.2
  55.5 2.1 copy-start.7
  57.7 115.9 %copy-start.1 = (f32[4,128,1536]{2,1,0:T(8,128)S(1)}, f32[4,128,1536]{2,1,0:T(8,128)}, u32[]{:S(2)}) copy-start(f32[4,128,1536]{2,1,0:T(8,128)} %all-gather.4.cloned.1.call-done) | copy-start | bytes 9437188
  61.1 122.0 %copy-start.5 = (s32[12]{0:T(128)S(1)}, s32[12]{0:T(128)}, u32[]{:S(2)}) copy-start(s32[12]{0:T(128)} %param.11) | copy-start | bytes 148
  210.7 5.5 %copy-start.8 = (f32[12,64,640]{2,1,0:T(8,128)S(1)}, f32[12,64,640]{2,1,0:T(8,128)}, u32[]{:S(2)}) copy-start(f32[12,64,640]{2,1,0:T(8,128)} %get-tuple-element.186) | copy-start | bytes 5898244 | tf_op jit(solution)/shard_map/while
  251.1 5.5 %copy-start.8 = (f32[12,64,640]{2,1,0:T(8,128)S(1)}, f32[12,64,640]{2,1,0:T(8,128)}, u32[]{:S(2)}) copy-start(f32[12,64,640]{2,1,0:T(8,128)} %get-tuple-element.186) | copy-start | bytes 5898244 | tf_op jit(solution)/shard_map/while
  291.4 5.5 %copy-start.8 = (f32[12,64,640]{2,1,0:T(8,128)S(1)}, f32[12,64,640]{2,1,0:T(8,128)}, u32[]{:S(2)}) copy-start(f32[12,64,640]{2,1,0:T(8,128)} %get-tuple-element.186) | copy-start | bytes 5898244 | tf_op jit(solution)/shard_map/while
  331.8 5.5 %copy-start.8 = (f32[12,64,640]{2,1,0:T(8,128)S(1)}, f32[12,64,640]{2,1,0:T(8,128)}, u32[]{:S(2)}) copy-start(f32[12,64,640]{2,1,0:T(8,128)} %get-tuple-element.186) | copy-start | bytes 5898244 | tf_op jit(solution)/shard_map/while
  357.0 2.8 copy-start
  377.6 4.2 copy-start.6
  377.6 40.2 %all-to-all-start = ((f32[4,4,16,1536]{3,2,0,1:T(8,128)}), f32[4,4,16,1536]{3,2,0,1:T(8,128)S(1)}, u32[]{:S(2)}, u32[]{:S(2)}) async-start(f32[4,4,16,1536]{3,2,0,1:T(8,128)} %copy.36), calls=%async_computation | async-start | bytes 3145728 | tf_op jit(solution)/shard_map/all_to_all | solution.py:119
  417.8 1.1 copy-start.4
  465.3 1.4 copy-start.3
Sparse Core Ops, SparseCore 0:
  9.7 14.8 all-gather.3
  26.1 13.2 all-gather.5
Sparse Core Ops, SparseCore 1:
  55.6 111.5 all-gather.7
